TPU v7x, 256 devices: a whole 4x4x8 slice. The times are simulated.
256 devices in a mesh: grp: 8 (over z), tp: 32 (over y, x, core).
Axes of the slice: x: 4, y: 4, z: 8, core: 2. Of those that a mesh axis runs over, the one named last changes fastest.
Arguments:
- hidden_in: bfloat16 [512, 4096], P('grp'), may hold values from -6 to 6
- norm_gain: float32 [4096], replicated, may hold values from 0.25 to 1.75
- head_weight: bfloat16 [4096, 128256], P('grp', 'tp'), may hold values from -1 to 1
- ffn_act: bfloat16 [512, 14336], P('grp', 'tp'), may hold values from -6 to 6
- labels: int32 [512], P('grp'), may hold values from 0 to 128255
- lengths: int32 [64], P('grp'), may hold values from 1 to 8
- proj_hidden: bfloat16 [4096, 64], replicated, may hold values from -0.09375 to 0.09375
- proj_vocab: bfloat16 [128256, 64], P('tp'), may hold values from -6 to 6
- proj_ffn: bfloat16 [14336, 64], P('tp'), may hold values from -0.046875 to 0.046875
- proj_down: bfloat16 [4096, 64], replicated, may hold values from -6 to 6
- store: bfloat16 [65536, 8192], P('grp', 'tp'), may hold values from -0.0625 to 0.0625
Outputs:
- scores: float32 [64, 65536], P('tp', 'grp')
All inputs are finite; a program needn't handle non-finite values.
Results may differ from a plain program's by a relative error of at most 0.012.
Values may be sent and summed in bfloat16 or wider, within the bound.
No kernel may reach another device: no remote copies, remote signals or barrier semaphores. Data moves between devices by JAX's collectives and lax.ppermute only.
A program may use at most 64 MiB of HBM per device.

v0:
```python
import jax
import jax.numpy as jnp
from jax import lax
from jax.sharding import PartitionSpec as P

epsilon = 1e-05
highest = lax.Precision.HIGHEST


def sent_to_all(value, axis):
    copies = jnp.broadcast_to(value, (lax.axis_size(axis), *value.shape))
    return lax.all_to_all(copies, axis, split_axis=0, concat_axis=0, tiled=True)


def over_copies(value, axis):
    everything = sent_to_all(value, axis)
    return jnp.max(everything, axis=0)


def of_everyone(value, axis):
    everything = sent_to_all(value, axis)
    return jnp.sum(everything, axis=0)


def packed_total(arrays, axis):
    vector, at, outs = (jnp.concatenate([a.reshape(-1) for a in arrays]), 0, [])
    so_far = of_everyone(vector, axis)
    for a in arrays:
        outs.append(so_far[at : at + a.size].reshape(a.shape))
        at += a.size
    return tuple(outs)


def laid_out(tiles, dim):
    shape = list(tiles.shape[1:])
    shape[dim] *= tiles.shape[0]
    return jnp.moveaxis(tiles, 0, dim).reshape(shape)


def gather_directly(value, axis, dim):
    tiles = sent_to_all(value, axis)
    return laid_out(tiles, dim)


def cut_along(value, dim, length):
    before, after = (value.shape[:dim], value.shape[dim + 1 :])
    return jnp.moveaxis(value.reshape(*before, length, -1, *after), dim, 0)


def sent_and_summed(value, axis, dim):
    tiles = cut_along(value, dim, lax.axis_size(axis))
    arrived = lax.all_to_all(tiles, axis, split_axis=0, concat_axis=0, tiled=True)
    return arrived.sum(axis=0)


def fold_rows(pieces, high_part, low_part):
    contract = (((0,), (0,)), ((), ()))
    upper = lax.dot_general(pieces, high_part, contract, preferred_element_type=jnp.float32)
    return upper + lax.dot_general(pieces, low_part, contract, preferred_element_type=jnp.float32)


def per_device(
    hidden_in,
    norm_gain,
    head_weight,
    ffn_act,
    labels,
    lengths,
    proj_hidden,
    proj_vocab,
    proj_ffn,
    proj_down,
    store,
):
    token_count, model_width = hidden_in.shape
    query_here = lengths.shape[0]
    seq_span = token_count // query_here
    rows_owned, vocab_owned = head_weight.shape
    rank_size = proj_hidden.shape[1]
    group_index = lax.axis_index("grp")
    vocab_index = lax.axis_index("tp")
    wide_hidden = hidden_in.astype(jnp.float32)
    inverse = lax.rsqrt(jnp.mean(wide_hidden * wide_hidden, axis=1, keepdims=True) + epsilon)
    unit_hidden = wide_hidden * inverse
    normed = (norm_gain * unit_hidden).astype(jnp.bfloat16)
    gained_down = norm_gain[:, None] * proj_down.astype(jnp.float32)
    down_high = gained_down.astype(jnp.bfloat16)
    down_low = (gained_down - down_high.astype(jnp.float32)).astype(jnp.bfloat16)
    spread = lax.all_to_all(normed, "grp", split_axis=1, concat_axis=0, tiled=True)
    logits = lax.psum_scatter(
        jnp.dot(spread, head_weight, preferred_element_type=jnp.float32),
        "grp",
        scatter_dimension=0,
        tiled=True,
    )
    local_max = jnp.max(logits, axis=1)
    peak = over_copies(local_max, "tp")
    denominator = of_everyone(jnp.sum(jnp.exp(logits - peak[:, None]), axis=1), "tp")
    probs = jnp.exp(logits - peak[:, None]) / denominator[:, None]
    positions = lax.broadcasted_iota(jnp.int32, (token_count,), 0) % seq_span
    valid = positions < jnp.repeat(lengths, seq_span)
    vocab_ids = vocab_index * vocab_owned + lax.broadcasted_iota(jnp.int32, (1, vocab_owned), 1)
    onehot = (labels[:, None] == vocab_ids).astype(jnp.float32)
    grads = jnp.where(valid[:, None], probs - onehot, 0.0).astype(jnp.bfloat16)
    own_high = lax.dynamic_slice_in_dim(down_high, group_index * rows_owned, rows_owned, 0)
    own_low = lax.dynamic_slice_in_dim(down_low, group_index * rows_owned, rows_owned, 0)
    local_fold = fold_rows(head_weight, own_high, own_low)
    folded_sum = lax.psum(local_fold, "grp")
    down_sum = jnp.dot(grads.astype(jnp.float32), folded_sum, precision=highest)
    head_side = jnp.dot(grads, proj_vocab, preferred_element_type=jnp.float32)
    label_dot = jnp.sum(grads.astype(jnp.float32) * logits, axis=1)
    ffn_side = jnp.dot(ffn_act, proj_ffn, preferred_element_type=jnp.float32)
    head_side, down_sum, label_dot, ffn_side = packed_total(
        (head_side, down_sum, label_dot, ffn_side), "tp"
    )
    hidden_side = jnp.dot(normed, proj_hidden, preferred_element_type=jnp.float32)
    unit_down = jnp.dot(unit_hidden, proj_down.astype(jnp.float32), precision=highest)
    down_side = inverse * (down_sum - (label_dot / model_width)[:, None] * unit_down)
    shaped = (query_here, seq_span, rank_size)
    first_outer = jnp.einsum("spa,spb->sab", hidden_side.reshape(shaped), head_side.reshape(shaped))
    second_outer = jnp.einsum("spa,spb->sab", ffn_side.reshape(shaped), down_side.reshape(shaped))
    queries = jnp.concatenate(
        [first_outer.reshape(query_here, -1), second_outer.reshape(query_here, -1)], axis=1
    ).astype(jnp.bfloat16)
    feature_owned = store.shape[1]
    own_queries = lax.dynamic_slice_in_dim(queries, vocab_index * feature_owned, feature_owned, 1)
    every_query = gather_directly(own_queries, "grp", 0)
    return sent_and_summed(
        lax.dot_general(
            every_query, store, (((1,), (1,)), ((), ())), preferred_element_type=jnp.float32
        ),
        "tp",
        0,
    )


def solution(mesh):
    return jax.shard_map(
        per_device,
        mesh=mesh,
        in_specs=(
            P("grp", None),
            P(),
            P("grp", "tp"),
            P("grp", "tp"),
            P("grp"),
            P("grp"),
            P(),
            P("tp", None),
            P("tp", None),
            P(),
            P("grp", "tp"),
        ),
        out_specs=P("tp", "grp"),
        check_vma=False,
    )
```

profile of v0, /device:TPU:1, one launch (start us, length us, event | category | flops | bytes accessed | tf_op | source)
XLA Modules:
  0.0 308.6 jit_solution(2016261024021584329)
XLA Ops:
  6.5 1.3 fusion.10
  7.9 1.2 fusion.9
  9.1 24.9 %all_to_all.47 = bf16[64,8,512]{2,0,1:T(8,128)(2,1)S(1)} all-to-all(bf16[64,8,512]{2,0,1:T(8,128)(2,1)S(1)} %bitcast.38), channel_id=1, replica_groups=mesh['grp'=8,'tp'=32] {'grp'}, dimensions={1} | all-to-all | bytes 1048576 | tf_op jit(solution)/shard_map/all_to_all | solution.py:89
  34.1 7.8 %fusion.25 = f32[512,4008]{1,0:T(8,128)} fusion(bf16[512,512]{1,0:T(8,128)(2,1)S(1)} %bitcast.37, bf16[512,4008]{0,1:T(8,128)(2,1)} %param.13), kind=kOutput, calls=%fused_computation.42 | convolution fusion | flops 2101346304 | bytes 12836864 | tf_op jit(solution)/shard_map/dot_general | solution.py:91
  42.0 1.0 copy-done.3
  43.1 3.7 %fusion.17 = f32[64,4008]{1,0:T(8,128)S(1)} fusion(bf16[512,4008]{0,1:T(8,128)(2,1)} %param.13, bf16[4096,64]{0,1:T(8,128)(2,1)S(1)} %get-tuple-element.8, s32[]{:T(128)S(6)} %select_n.24), kind=kOutput, calls=%fused_computation.30 | convolution fusion | flops 262668288 | bytes 5195780 | tf_op jit(solution)/shard_map/dot_general | solution.py:58
  46.8 2.3 fusion
  49.5 85.5 %reduce-scatter.2.cloned.1.call-done = f32[64,4008]{1,0:T(8,128)} async-done(((f32[512,4008]{1,0:T(8,128)}), f32[64,4008]{1,0:T(8,128)}) %reduce-scatter.2.cloned.1.call-update) | async-done | bytes 1026064 | tf_op jit(solution)/shard_map/reduce_scatter | solution.py:90
  134.9 1.4 reduce_max.18
  136.3 0.6 broadcast_in_dim.38
  136.9 7.6 %all-to-all-start.1 = ((f32[32,1,64]{2,1,0:T(1,128)}), f32[32,1,64]{2,1,0:T(1,128)S(1)}, u32[]{:S(2)}, u32[]{:S(2)}) async-start(f32[32,1,64]{2,1,0:T(1,128)} %broadcast_in_dim.38), calls=%async_computation.2 | async-start | bytes 32768 | tf_op jit(solution)/shard_map/all_to_all | solution.py:12
  144.5 6.9 %all-to-all-done.1 = f32[32,1,64]{2,1,0:T(1,128)S(1)} async-done(((f32[32,1,64]{2,1,0:T(1,128)}), f32[32,1,64]{2,1,0:T(1,128)S(1)}, u32[]{:S(2)}, u32[]{:S(2)}) %all-to-all-start.1) | async-done | bytes 8224 | tf_op jit(solution)/shard_map/all_to_all | solution.py:12
  151.4 1.5 fusion.11
  153.0 0.6 broadcast_in_dim.39
  153.6 4.1 %all-to-all-start.2 = ((f32[32,1,64]{2,1,0:T(1,128)}), f32[32,1,64]{2,1,0:T(1,128)S(1)}, u32[]{:S(2)}, u32[]{:S(2)}) async-start(f32[32,1,64]{2,1,0:T(1,128)} %broadcast_in_dim.39), calls=%async_computation.3 | async-start | bytes 32768 | tf_op jit(solution)/shard_map/all_to_all | solution.py:12
  157.8 6.9 %all-to-all-done.2 = f32[32,1,64]{2,1,0:T(1,128)S(1)} async-done(((f32[32,1,64]{2,1,0:T(1,128)}), f32[32,1,64]{2,1,0:T(1,128)S(1)}, u32[]{:S(2)}, u32[]{:S(2)}) %all-to-all-start.2) | async-done | bytes 8224 | tf_op jit(solution)/shard_map/all_to_all | solution.py:12
  164.8 1.8 multiply_reduce_fusion
  166.6 0.3 fusion.26
  166.9 40.7 %all-reduce.2.cloned.1.call-done = f32[4008,64]{0,1:T(8,128)} async-done(((f32[4008,64]{0,1:T(8,128)}), f32[4008,64]{0,1:T(8,128)}) %all-reduce.2.cloned.1.call-update) | async-done | bytes 1026064 | tf_op jit(solution)/shard_map/psum | solution.py:108
  207.6 1.9 fusion.27
  209.7 2.0 broadcast_in_dim.41
  211.6 11.9 %all-to-all-start.3 = ((f32[32,1,12352]{2,1,0:T(1,128)}), f32[32,1,12352]{2,1,0:T(1,128)S(1)}, u32[]{:S(2)}, u32[]{:S(2)}) async-start(f32[32,1,12352]{2,1,0:T(1,128)} %broadcast_in_dim.41), calls=%async_computation.4 | async-start | bytes 3178496 | tf_op jit(solution)/shard_map/all_to_all | solution.py:12
  223.6 22.4 %all-to-all-done.3 = f32[32,1,12352]{2,1,0:T(1,128)S(1)} async-done(((f32[32,1,12352]{2,1,0:T(1,128)}), f32[32,1,12352]{2,1,0:T(1,128)S(1)}, u32[]{:S(2)}, u32[]{:S(2)}) %all-to-all-start.3) | async-done | bytes 1581088 | tf_op jit(solution)/shard_map/all_to_all | solution.py:12
  246.0 0.9 reduce_sum.58
  247.1 0.6 convolution_convert_fusion.1
  248.0 1.8 fusion.8
  249.8 0.2 fusion.29
  250.3 10.6 %all_to_all.48 = bf16[8,8,256]{2,1,0:T(8,128)(2,1)S(1)} all-to-all(bf16[8,8,256]{2,1,0:T(8,128)(2,1)S(1)} %broadcast_in_dim.42), channel_id=1, replica_groups=mesh['grp'=8,'tp'=32] {'grp'}, dimensions={0} | all-to-all | bytes 65536 | tf_op jit(solution)/shard_map/all_to_all | solution.py:12
  260.8 3.6 %fusion.1 = f32[32,2,8192]{2,0,1:T(8,128)S(1)} fusion(bf16[8192,256]{1,0:T(8,128)(2,1)} %param.21, bf16[32,2,256]{2,1,0:T(2,128)(2,1)S(1)} %dot_general.45), kind=kOutput, calls=%fused_computation.2 | convolution fusion | flops 268435456 | bytes 6324224 | tf_op jit(solution)/shard_map/dot_general | solution.py:129
  264.4 1.6 copy.26
  266.0 34.4 %all_to_all.49 = f32[32,2,8192]{2,1,0:T(2,128)S(1)} all-to-all(f32[32,2,8192]{2,1,0:T(2,128)S(1)} %copy.26), channel_id=1, replica_groups=mesh['grp'=8,'tp'=32] {'tp'}, dimensions={0} | all-to-all | bytes 4194304 | tf_op jit(solution)/shard_map/all_to_all | solution.py:52
  300.4 1.4 reduce_sum.59
  (48 shorter events, 1.7 us)
Async XLA Ops:
  6.5 240.6 %copy-start = (bf16[4096,64]{0,1:T(8,128)(2,1)S(1)}, bf16[4096,64]{0,1:T(8,128)(2,1)}, u32[]{:S(2)}) copy-start(bf16[4096,64]{0,1:T(8,128)(2,1)} %param.17) | copy-start | bytes 1572868
  6.5 128.4 %reduce-scatter.2.cloned.1.call-start = ((), (), s32[]{:S(2)}) async-start(), calls=%async_computation.7 | async-start | bytes 9437184 | tf_op jit(solution)/shard_map/reduce_scatter | solution.py:90
  41.9 1.0 copy-start.3
  41.9 1.0 copy-start.5
  41.9 165.7 %all-reduce.2.cloned.1.call-start = ((), (), s32[]{:S(2)}) async-start(), calls=%async_computation.8 | async-start | bytes 2097152 | tf_op jit(solution)/shard_map/psum | solution.py:108
  42.9 3.9 %copy-start.1 = (bf16[512,4008]{0,1:T(8,128)(2,1)S(1)}, bf16[512,4008]{0,1:T(8,128)(2,1)}, u32[]{:S(2)}) copy-start(bf16[512,4008]{0,1:T(8,128)(2,1)} %param.13) | copy-start | bytes 12312580
  46.7 2.4 copy-start.9
  46.7 2.6 copy-start.6
  46.8 2.6 copy-start.7
  46.8 118.0 %copy-start.8 = (s32[64]{0:T(128)S(1)}, s32[64]{0:T(128)}, u32[]{:S(2)}) copy-start(s32[64]{0:T(128)} %param.15) | copy-start | bytes 772
  49.1 117.4 %copy-start.4 = (bf16[4008,64]{0,1:T(8,128)(2,1)S(1)}, bf16[4008,64]{0,1:T(8,128)(2,1)}, u32[]{:S(2)}) copy-start(bf16[4008,64]{0,1:T(8,128)(2,1)} %param.18) | copy-start | bytes 1539076
  136.9 14.5 %all-to-all-start.1 = ((f32[32,1,64]{2,1,0:T(1,128)}), f32[32,1,64]{2,1,0:T(1,128)S(1)}, u32[]{:S(2)}, u32[]{:S(2)}) async-start(f32[32,1,64]{2,1,0:T(1,128)} %broadcast_in_dim.38), calls=%async_computation.2 | async-start | bytes 32768 | tf_op jit(solution)/shard_map/all_to_all | solution.py:12
  153.6 11.1 %all-to-all-start.2 = ((f32[32,1,64]{2,1,0:T(1,128)}), f32[32,1,64]{2,1,0:T(1,128)S(1)}, u32[]{:S(2)}, u32[]{:S(2)}) async-start(f32[32,1,64]{2,1,0:T(1,128)} %broadcast_in_dim.39), calls=%async_computation.3 | async-start | bytes 32768 | tf_op jit(solution)/shard_map/all_to_all | solution.py:12
  209.5 38.5 %copy-start.2 = (bf16[64,4096]{1,0:T(8,128)(2,1)S(1)}, bf16[64,4096]{1,0:T(8,128)(2,1)}, u32[]{:S(2)}) copy-start(bf16[64,4096]{1,0:T(8,128)(2,1)} %param.11) | copy-start | bytes 1572868
  211.6 34.4 %all-to-all-start.3 = ((f32[32,1,12352]{2,1,0:T(1,128)}), f32[32,1,12352]{2,1,0:T(1,128)S(1)}, u32[]{:S(2)}, u32[]{:S(2)}) async-start(f32[32,1,12352]{2,1,0:T(1,128)} %broadcast_in_dim.41), calls=%async_computation.4 | async-start | bytes 3178496 | tf_op jit(solution)/shard_map/all_to_all | solution.py:12
Sparse Core Ops, SparseCore 0:
  42.0 92.8 reduce-scatter.1
  137.3 70.2 all-reduce.1
where the time goes:
time: 309 us
  waiting for transfers between devices  162 us (52%)
  blocking collectives  69.8 us (23%)
  starting transfers between devices  23.7 us (8%)
  matrix products  22.3 us (7%)
  between operations  13.7 us (4%)
  other arithmetic  9.72 us (3%)
  local copies, waits for them, and re-layouts  7.04 us (2%)
    reduce_scatter x1, waiting for transfers between devices, per_device(): lax.psum_scatter(jnp.dot(spread, head_weight, preferred_element_type=jnp....  85.5 us
    psum x1, waiting for transfers between devices, per_device(): folded_sum = lax.psum(local_fold, 'grp')  40.7 us
    all_to_all x3, waiting for transfers between devices, sent_to_all(): return lax.all_to_all(copies, axis, split_axis=0, concat_axis=0, tiled=True)  36.2 us
    all_to_all x1, blocking collectives, sent_and_summed(): lax.all_to_all(tiles, axis, split_axis=0, concat_axis=0, tiled=True)  34.4 us
    all_to_all x1, blocking collectives, per_device(): lax.all_to_all(normed, 'grp', split_axis=1, concat_axis=0, tiled=True)  24.9 us
    all_to_all x3, starting transfers between devices, sent_to_all(): return lax.all_to_all(copies, axis, split_axis=0, concat_axis=0, tiled=True)  23.6 us
    all_to_all x1, blocking collectives, sent_to_all(): return lax.all_to_all(copies, axis, split_axis=0, concat_axis=0, tiled=True)  10.6 us
    dot_general x1, matrix products, per_device(): jnp.dot(spread, head_weight, preferred_element_type=jnp.float32)  7.81 us
  transfers between devices with their start and end apart: 5, of which 5 were waited for; matrix products, arithmetic and copies ran while one was open for 4% of the time, Pallas kernels for 0%

commit v1 on v0

--- a/solution.py
+++ b/solution.py
@@ -105,7 +105,11 @@
     own_high = lax.dynamic_slice_in_dim(down_high, group_index * rows_owned, rows_owned, 0)
     own_low = lax.dynamic_slice_in_dim(down_low, group_index * rows_owned, rows_owned, 0)
     local_fold = fold_rows(head_weight, own_high, own_low)
-    folded_sum = lax.psum(local_fold, "grp")
+    folded_sum = local_fold
+    for hop in (1, 2, 4):
+        folded_sum = folded_sum + lax.ppermute(
+            folded_sum, "grp", [(dev, dev ^ hop) for dev in range(8)]
+        )
     down_sum = jnp.dot(grads.astype(jnp.float32), folded_sum, precision=highest)
     head_side = jnp.dot(grads, proj_vocab, preferred_element_type=jnp.float32)
     label_dot = jnp.sum(grads.astype(jnp.float32) * logits, axis=1)

time: 309 us -> 362 us (1.17)
  waiting for transfers between devices: 162 us -> 206 us
  blocking collectives: 69.8 us -> 79.8 us
    ppermute x0 -> x3, waiting for transfers between devices: none -> 107 us  [per_device(): lax.ppermute(folded_sum, 'grp', [(dev, dev ^ hop) for dev in range(8)])]
    psum x1 -> x0, waiting for transfers between devices: 40.7 us -> none  [per_device(): folded_sum = lax.psum(local_fold, 'grp')]
    reduce_scatter x1, waiting for transfers between devices: 85.5 us -> 63.2 us  [per_device(): lax.psum_scatter(jnp.dot(spread, head_weight, preferred_element_type=jnp....]
    all_to_all x1, blocking collectives: 10.6 us -> 20.5 us  [sent_to_all(): return lax.all_to_all(copies, axis, split_axis=0, concat_axis=0, tiled=True)]
    all_to_all x3, starting transfers between devices: 23.6 us -> 16.8 us  [sent_to_all(): return lax.all_to_all(copies, axis, split_axis=0, concat_axis=0, tiled=True)]
    ppermute x0 -> x3, starting transfers between devices: none -> 3.85 us  [per_device(): lax.ppermute(folded_sum, 'grp', [(dev, dev ^ hop) for dev in range(8)])]
  transfers between devices with their start and end apart: 5 -> 7, of which waited for: 5 -> 6; matrix products, arithmetic and copies ran while one was open for 4% -> 4% of each run, Pallas kernels for 0% -> 0%
where the time goes in v1:
time: 362 us; the launch traced here: 361 us
  waiting for transfers between devices  206 us (57%)
  blocking collectives  79.8 us (22%)
  matrix products  22.3 us (6%)
  starting transfers between devices  20.7 us (6%)
  between operations  13.7 us (4%)
  other arithmetic  11.2 us (3%)
  local copies, waits for them, and re-layouts  7.09 us (2%)
    ppermute x3, waiting for transfers between devices, per_device(): lax.ppermute(folded_sum, 'grp', [(dev, dev ^ hop) for dev in range(8)])  107 us
    reduce_scatter x1, waiting for transfers between devices, per_device(): lax.psum_scatter(jnp.dot(spread, head_weight, preferred_element_type=jnp....  63.2 us
    all_to_all x3, waiting for transfers between devices, sent_to_all(): return lax.all_to_all(copies, axis, split_axis=0, concat_axis=0, tiled=True)  36.3 us
    all_to_all x1, blocking collectives, sent_and_summed(): lax.all_to_all(tiles, axis, split_axis=0, concat_axis=0, tiled=True)  34.4 us
    all_to_all x1, blocking collectives, per_device(): lax.all_to_all(normed, 'grp', split_axis=1, concat_axis=0, tiled=True)  24.9 us
    all_to_all x1, blocking collectives, sent_to_all(): return lax.all_to_all(copies, axis, split_axis=0, concat_axis=0, tiled=True)  20.5 us
    all_to_all x3, starting transfers between devices, sent_to_all(): return lax.all_to_all(copies, axis, split_axis=0, concat_axis=0, tiled=True)  16.8 us
    dot_general x1, matrix products, per_device(): jnp.dot(spread, head_weight, preferred_element_type=jnp.float32)  7.81 us
  transfers between devices with their start and end apart: 7, of which 6 were waited for; matrix products, arithmetic and copies ran while one was open for 4% of the time, Pallas kernels for 0%

profile of v1, /device:TPU:1, one launch (start us, length us, event | category | flops | bytes accessed | tf_op | source)
XLA Modules:
  0.0 361.1 jit_solution(4116357961379938424)
XLA Ops:
  6.5 1.3 fusion.10
  7.9 1.2 fusion.9
  9.1 24.9 %all_to_all.47 = bf16[64,8,512]{2,0,1:T(8,128)(2,1)S(1)} all-to-all(bf16[64,8,512]{2,0,1:T(8,128)(2,1)S(1)} %bitcast.37), channel_id=1, replica_groups=mesh['grp'=8,'tp'=32] {'grp'}, dimensions={1} | all-to-all | bytes 1048576 | tf_op jit(solution)/shard_map/all_to_all | solution.py:89
  34.1 7.8 %fusion.27 = f32[512,4008]{1,0:T(8,128)} fusion(bf16[512,512]{1,0:T(8,128)(2,1)S(1)} %bitcast.36, bf16[512,4008]{0,1:T(8,128)(2,1)} %param.13), kind=kOutput, calls=%fused_computation.44 | convolution fusion | flops 2101346304 | bytes 12836864 | tf_op jit(solution)/shard_map/dot_general | solution.py:91
  41.9 1.0 copy-done.3
  43.1 3.7 %fusion.19 = f32[64,4008]{1,0:T(8,128)S(1)} fusion(bf16[512,4008]{0,1:T(8,128)(2,1)} %param.13, bf16[4096,64]{0,1:T(8,128)(2,1)S(1)} %get-tuple-element.8, s32[]{:T(128)S(6)} %select_n.24), kind=kOutput, calls=%fused_computation.32 | convolution fusion | flops 262668288 | bytes 5195780 | tf_op jit(solution)/shard_map/dot_general | solution.py:58
  46.8 1.4 fusion
  48.3 40.1 %collective-permute-done = f32[4008,64]{0,1:T(8,128)S(1)} collective-permute-done((f32[4008,64]{0,1:T(8,128)S(1)}, f32[4008,64]{0,1:T(8,128)S(1)}, u32[]{:S(2)}, u32[]{:S(2)}) %collective-permute-start) | collective-permute-done | bytes 1026080 | tf_op jit(solution)/shard_map/ppermute | solution.py:110
  89.0 66.6 %collective-permute-done.1 = f32[4008,64]{0,1:T(8,128)} collective-permute-done((f32[4008,64]{0,1:T(8,128)S(1)}, f32[4008,64]{0,1:T(8,128)}, u32[]{:S(2)}, u32[]{:S(2)}) %collective-permute-start.1) | collective-permute-done | bytes 1026080 | tf_op jit(solution)/shard_map/ppermute | solution.py:110
  155.6 1.3 add.65
  156.9 3.7 %collective-permute-start.2 = (f32[4008,64]{0,1:T(8,128)S(1)}, f32[4008,64]{0,1:T(8,128)}, u32[]{:S(2)}, u32[]{:S(2)}) collective-permute-start(f32[4008,64]{0,1:T(8,128)S(1)} %add.65), channel_id=1, source_target_pairs={{0,128},{32,160},{64,192},{96,224},{128,0},{160,32},{192,64},{224,... | collective-permute-start | bytes 3078152 | tf_op jit(solution)/shard_map/ppermute | solution.py:110
  160.6 63.2 %reduce-scatter.2.cloned.1.call-done = f32[64,4008]{1,0:T(8,128)} async-done(((f32[512,4008]{1,0:T(8,128)}), f32[64,4008]{1,0:T(8,128)}) %reduce-scatter.2.cloned.1.call-update) | async-done | bytes 1026064 | tf_op jit(solution)/shard_map/reduce_scatter | solution.py:90
  223.7 1.4 reduce_max.18
  225.1 0.6 broadcast_in_dim.38
  225.7 8.4 %all-to-all-start.1 = ((f32[32,1,64]{2,1,0:T(1,128)}), f32[32,1,64]{2,1,0:T(1,128)S(1)}, u32[]{:S(2)}, u32[]{:S(2)}) async-start(f32[32,1,64]{2,1,0:T(1,128)} %broadcast_in_dim.38), calls=%async_computation.2 | async-start | bytes 32768 | tf_op jit(solution)/shard_map/all_to_all | solution.py:12
  234.2 6.9 %all-to-all-done.1 = f32[32,1,64]{2,1,0:T(1,128)S(1)} async-done(((f32[32,1,64]{2,1,0:T(1,128)}), f32[32,1,64]{2,1,0:T(1,128)S(1)}, u32[]{:S(2)}, u32[]{:S(2)}) %all-to-all-start.1) | async-done | bytes 8224 | tf_op jit(solution)/shard_map/all_to_all | solution.py:12
  241.1 1.5 fusion.13
  243.3 4.1 %all-to-all-start.2 = ((f32[32,1,64]{2,1,0:T(1,128)}), f32[32,1,64]{2,1,0:T(1,128)S(1)}, u32[]{:S(2)}, u32[]{:S(2)}) async-start(f32[32,1,64]{2,1,0:T(1,128)} %broadcast_in_dim.39), calls=%async_computation.3 | async-start | bytes 32768 | tf_op jit(solution)/shard_map/all_to_all | solution.py:12
  247.5 6.9 %all-to-all-done.2 = f32[32,1,64]{2,1,0:T(1,128)S(1)} async-done(((f32[32,1,64]{2,1,0:T(1,128)}), f32[32,1,64]{2,1,0:T(1,128)S(1)}, u32[]{:S(2)}, u32[]{:S(2)}) %all-to-all-start.2) | async-done | bytes 8224 | tf_op jit(solution)/shard_map/all_to_all | solution.py:12
  254.4 1.8 multiply_reduce_fusion
  256.2 1.3 fusion.28
  257.6 1.9 fusion.11
  259.7 2.0 broadcast_in_dim.41
  261.7 4.3 %all-to-all-start.3 = ((f32[32,1,12352]{2,1,0:T(1,128)}), f32[32,1,12352]{2,1,0:T(1,128)S(1)}, u32[]{:S(2)}, u32[]{:S(2)}) async-start(f32[32,1,12352]{2,1,0:T(1,128)} %broadcast_in_dim.41), calls=%async_computation.4 | async-start | bytes 3178496 | tf_op jit(solution)/shard_map/all_to_all | solution.py:12
  266.0 22.5 %all-to-all-done.3 = f32[32,1,12352]{2,1,0:T(1,128)S(1)} async-done(((f32[32,1,12352]{2,1,0:T(1,128)}), f32[32,1,12352]{2,1,0:T(1,128)S(1)}, u32[]{:S(2)}, u32[]{:S(2)}) %all-to-all-start.3) | async-done | bytes 1581088 | tf_op jit(solution)/shard_map/all_to_all | solution.py:12
  288.5 0.9 reduce_sum.58
  290.5 1.8 fusion.8
  292.7 20.5 %all_to_all.48 = bf16[8,8,256]{2,1,0:T(8,128)(2,1)S(1)} all-to-all(bf16[8,8,256]{2,1,0:T(8,128)(2,1)S(1)} %broadcast_in_dim.42), channel_id=1, replica_groups=mesh['grp'=8,'tp'=32] {'grp'}, dimensions={0} | all-to-all | bytes 65536 | tf_op jit(solution)/shard_map/all_to_all | solution.py:12
  313.2 3.6 fusion.1
  316.8 1.6 copy.26
  318.4 34.4 %all_to_all.49 = f32[32,2,8192]{2,1,0:T(2,128)S(1)} all-to-all(f32[32,2,8192]{2,1,0:T(2,128)S(1)} %copy.26), channel_id=1, replica_groups=mesh['grp'=8,'tp'=32] {'tp'}, dimensions={0} | all-to-all | bytes 4194304 | tf_op jit(solution)/shard_map/all_to_all | solution.py:52
  352.8 1.4 reduce_sum.59
  (51 shorter events, 3.4 us)
Async XLA Ops:
  6.5 283.0 %copy-start = (bf16[4096,64]{0,1:T(8,128)(2,1)S(1)}, bf16[4096,64]{0,1:T(8,128)(2,1)}, u32[]{:S(2)}) copy-start(bf16[4096,64]{0,1:T(8,128)(2,1)} %param.17) | copy-start | bytes 1572868
  6.5 217.2 %reduce-scatter.2.cloned.1.call-start = ((), (), s32[]{:S(2)}) async-start(), calls=%async_computation.7 | async-start | bytes 9437184 | tf_op jit(solution)/shard_map/reduce_scatter | solution.py:90
  41.9 1.0 copy-start.3
  41.9 1.0 copy-start.4
  42.9 3.8 %copy-start.1 = (bf16[512,4008]{0,1:T(8,128)(2,1)S(1)}, bf16[512,4008]{0,1:T(8,128)(2,1)}, u32[]{:S(2)}) copy-start(bf16[512,4008]{0,1:T(8,128)(2,1)} %param.13) | copy-start | bytes 12312580
  46.7 41.9 %copy-start.8 = (s32[8]{0:T(128)S(1)}, s32[8]{0:T(128)}, u32[]{:S(2)}) copy-start(s32[8]{0:T(128)} %param.16) | copy-start | bytes 100
  46.8 42.1 %copy-start.5 = (bf16[64,448]{1,0:T(8,128)(2,1)S(1)}, bf16[64,448]{1,0:T(8,128)(2,1)}, u32[]{:S(2)}) copy-start(bf16[64,448]{1,0:T(8,128)(2,1)} %param.14) | copy-start | bytes 172036
  46.8 42.1 %copy-start.6 = (bf16[448,64]{0,1:T(8,128)(2,1)S(1)}, bf16[448,64]{0,1:T(8,128)(2,1)}, u32[]{:S(2)}) copy-start(bf16[448,64]{0,1:T(8,128)(2,1)} %param.19) | copy-start | bytes 172036
  48.1 206.3 %copy-start.7 = (s32[64]{0:T(128)S(1)}, s32[64]{0:T(128)}, u32[]{:S(2)}) copy-start(s32[64]{0:T(128)} %param.15) | copy-start | bytes 772
  48.2 40.2 %collective-permute-start = (f32[4008,64]{0,1:T(8,128)S(1)}, f32[4008,64]{0,1:T(8,128)S(1)}, u32[]{:S(2)}, u32[]{:S(2)}) collective-permute-start(f32[4008,64]{0,1:T(8,128)S(1)} %fusion), channel_id=1, source_target_pairs={{0,32},{32,0},{64,96},{96,64},{128,160},{160,128},{192,224},{224,1... | collective-permute-start | bytes 3078152 | tf_op jit(solution)/shard_map/ppermute | solution.py:110
  88.6 67.0 %collective-permute-start.1 = (f32[4008,64]{0,1:T(8,128)S(1)}, f32[4008,64]{0,1:T(8,128)}, u32[]{:S(2)}, u32[]{:S(2)}) collective-permute-start(f32[4008,64]{0,1:T(8,128)S(1)} %add.64), channel_id=1, source_target_pairs={{0,64},{32,96},{64,0},{96,32},{128,192},{160,224},{192,128},{224,1... | collective-permute-start | bytes 3078152 | tf_op jit(solution)/shard_map/ppermute | solution.py:110
  156.9 100.7 %collective-permute-start.2 = (f32[4008,64]{0,1:T(8,128)S(1)}, f32[4008,64]{0,1:T(8,128)}, u32[]{:S(2)}, u32[]{:S(2)}) collective-permute-start(f32[4008,64]{0,1:T(8,128)S(1)} %add.65), channel_id=1, source_target_pairs={{0,128},{32,160},{64,192},{96,224},{128,0},{160,32},{192,64},{224,... | collective-permute-start | bytes 3078152 | tf_op jit(solution)/shard_map/ppermute | solution.py:110
  225.7 15.3 %all-to-all-start.1 = ((f32[32,1,64]{2,1,0:T(1,128)}), f32[32,1,64]{2,1,0:T(1,128)S(1)}, u32[]{:S(2)}, u32[]{:S(2)}) async-start(f32[32,1,64]{2,1,0:T(1,128)} %broadcast_in_dim.38), calls=%async_computation.2 | async-start | bytes 32768 | tf_op jit(solution)/shard_map/all_to_all | solution.py:12
  243.3 11.1 %all-to-all-start.2 = ((f32[32,1,64]{2,1,0:T(1,128)}), f32[32,1,64]{2,1,0:T(1,128)S(1)}, u32[]{:S(2)}, u32[]{:S(2)}) async-start(f32[32,1,64]{2,1,0:T(1,128)} %broadcast_in_dim.39), calls=%async_computation.3 | async-start | bytes 32768 | tf_op jit(solution)/shard_map/all_to_all | solution.py:12
  259.5 30.9 %copy-start.2 = (bf16[64,4096]{1,0:T(8,128)(2,1)S(1)}, bf16[64,4096]{1,0:T(8,128)(2,1)}, u32[]{:S(2)}) copy-start(bf16[64,4096]{1,0:T(8,128)(2,1)} %param.11) | copy-start | bytes 1572868
  261.7 26.8 %all-to-all-start.3 = ((f32[32,1,12352]{2,1,0:T(1,128)}), f32[32,1,12352]{2,1,0:T(1,128)S(1)}, u32[]{:S(2)}, u32[]{:S(2)}) async-start(f32[32,1,12352]{2,1,0:T(1,128)} %broadcast_in_dim.41), calls=%async_computation.4 | async-start | bytes 3178496 | tf_op jit(solution)/shard_map/all_to_all | solution.py:12
Sparse Core Ops, SparseCore 0:
  42.0 181.6 reduce-scatter.1
